TPU v7x, 256 devices: a whole 4x4x8 slice. The times are simulated.
256 devices in a mesh: kv: 32 (over z, y), tp: 8 (over x, core).
Axes of the slice: x: 4, y: 4, z: 8, core: 2. Of those that a mesh axis runs over, the one named last changes fastest.
Arguments:
- queries: bfloat16 [8, 4, 128, 128], P(None, None, 'tp'), may hold values from -30 to 30
- cache_keys: bfloat16 [8, 8192, 8, 128], P(None, 'kv', 'tp'), may hold values from -4 to 4
- cache_values: bfloat16 [8, 8192, 8, 128], P(None, 'kv', 'tp'), may hold values from -6 to 6
- new_keys: bfloat16 [8, 4, 8, 128], P(None, None, 'tp'), may hold values from -6 to 6
- new_values: bfloat16 [8, 4, 8, 128], P(None, None, 'tp'), may hold values from -6 to 6
- lengths: int32 [8], replicated, may hold values from 512 to 8192
- residual: bfloat16 [32, 16384], P(None, 'kv'), may hold values from -4 to 4
- out_weight: bfloat16 [16384, 16384], P('tp', 'kv'), may hold values from -0.1875 to 0.1875
- norm_gain: bfloat16 [16384], P('kv'), may hold values from 0.099609375 to 1.8984375
- gate_weight: bfloat16 [16384, 26624], P('kv', 'tp'), may hold values from -0.046875 to 0.046875
- up_weight: bfloat16 [16384, 26624], P('kv', 'tp'), may hold values from -0.046875 to 0.046875
- down_weight: bfloat16 [26624, 16384], P('tp', 'kv'), may hold values from -0.0546875 to 0.0546875
Outputs:
- after_attention: bfloat16 [32, 16384], P(None, 'kv')
- layer_out: bfloat16 [32, 16384], P('tp', 'kv')
All inputs are finite; a program needn't handle non-finite values.
Results may differ from a plain program's by a relative error of at most 0.019.
Values may be sent and summed in bfloat16 or wider, within the bound.
A program may use at most 64 MiB of HBM per device.

v0:
```python
import math
import jax
import jax.numpy as jnp
from jax import lax
from jax.sharding import PartitionSpec as P


def turned_gather(arrays, axis, dims):
    turned = [jnp.moveaxis(a, dim, 0) for a, dim in zip(arrays, dims)]
    both = jnp.concatenate([t.reshape(len(t), -1) for t in turned], axis=1)
    result, at, done = (lax.all_gather(both, axis, axis=0, tiled=True), 0, [])
    for t, dim in zip(turned, dims):
        piece = result[:, at : at + t[0].size].reshape(-1, *t.shape[1:])
        done.append(jnp.moveaxis(piece, 0, dim))
        at += t[0].size
    return tuple(done)


def sent_to_all(array, axis):
    copies = jnp.broadcast_to(array, (lax.axis_size(axis), *array.shape))
    return lax.all_to_all(copies, axis, split_axis=0, concat_axis=0, tiled=True)


def of_everyone(array, axis):
    everything = sent_to_all(array, axis)
    return jnp.sum(everything, axis=0)


def split_up(array, dim, peers):
    before, after = (array.shape[:dim], array.shape[dim + 1 :])
    return jnp.moveaxis(array.reshape(*before, peers, -1, *after), dim, 0)


def summed_on_arrival(array, axis, dim):
    peers = lax.axis_size(axis)
    tiles = lax.all_to_all(split_up(array, dim, peers), axis, 0, 0, tiled=True)
    return jnp.sum(tiles, axis=0)


def side_by_side(arrays, axis, dim, along):
    widths = [a.shape[along] for a in arrays]
    both = jnp.concatenate(arrays, axis=along)
    result = summed_on_arrival(both, axis, dim)
    return tuple(jnp.split(result, [sum(widths[:k]) for k in range(1, len(widths))], axis=along))


def laid_out(tiles, dim):
    dims = list(tiles.shape[1:])
    dims[dim] *= tiles.shape[0]
    return jnp.moveaxis(tiles, 0, dim).reshape(dims)


def collect(array, axis, dim):
    return laid_out(sent_to_all(array, axis), dim)


def fold_sources(received):
    source_max, source_total, source_sum = received
    row_max = jnp.max(source_max, axis=0)
    factor = jnp.exp(source_max - row_max[None])
    return (
        row_max,
        jnp.sum(source_total * factor, axis=0),
        jnp.sum(source_sum * factor[..., None], axis=0),
    )


def local(
    queries,
    cache_keys,
    cache_values,
    new_keys,
    new_values,
    lengths,
    residual,
    out_weight,
    norm_gain,
    gate_weight,
    up_weight,
    down_weight,
):
    seq_count, step_count, heads_local, head_dim = queries.shape
    ctx_local = cache_keys.shape[1]
    kv_local = cache_keys.shape[2]
    group_size = heads_local // kv_local
    scaling = 1.0 / math.sqrt(head_dim)
    grouped = queries.reshape(seq_count, step_count, kv_local, group_size, head_dim)
    scores = (
        jnp.einsum("stgjd,scgd->sgjtc", grouped, cache_keys, preferred_element_type=jnp.float32)
        * scaling
    )
    position = lax.axis_index("kv") * ctx_local + lax.iota(jnp.int32, ctx_local)
    in_range = (position[None, :] < lengths[:, None])[:, None, None, None, :]
    masked = jnp.where(in_range, scores, -1e30)
    local_max = jnp.max(masked, axis=-1)
    weights = jnp.where(in_range, jnp.exp(masked - local_max[..., None]), 0.0)
    local_total = jnp.sum(weights, axis=-1)
    local_sum = jnp.einsum(
        "sgjtc,scgd->sgjtd",
        weights.astype(jnp.bfloat16),
        cache_values,
        preferred_element_type=jnp.float32,
    )
    pieces = lax.axis_size("kv")
    row_max, row_total, row_sum = fold_sources(
        (
            lax.all_to_all(
                local_max.reshape(pieces, -1), "kv", split_axis=0, concat_axis=0, tiled=True
            ),
            lax.all_to_all(
                local_total.reshape(pieces, -1), "kv", split_axis=0, concat_axis=0, tiled=True
            ),
            lax.all_to_all(
                local_sum.reshape(pieces, -1, head_dim),
                "kv",
                split_axis=0,
                concat_axis=0,
                tiled=True,
            ),
        )
    )
    gathered_max, gathered_total, gathered_sum = turned_gather(
        (row_max, row_total, row_sum), "kv", (0, 0, 0)
    )
    cache_max = gathered_max.reshape(local_max.shape)
    cache_total = gathered_total.reshape(local_total.shape)
    cache_sum = gathered_sum.reshape(local_sum.shape)
    fresh_scores = (
        jnp.einsum("stgjd,sugd->sgjtu", grouped, new_keys, preferred_element_type=jnp.float32)
        * scaling
    )
    causal = lax.iota(jnp.int32, step_count)[:, None] >= lax.iota(jnp.int32, step_count)[None, :]
    fresh_scores = jnp.where(causal, fresh_scores, -1e30)
    row_top = jnp.maximum(cache_max, jnp.max(fresh_scores, axis=-1))
    carried = jnp.exp(cache_max - row_top)
    fresh_weights = jnp.where(causal, jnp.exp(fresh_scores - row_top[..., None]), 0.0)
    denominator = cache_total * carried + jnp.sum(fresh_weights, axis=-1)
    numerator = cache_sum * carried[..., None] + jnp.einsum(
        "sgjtu,sugd->sgjtd",
        fresh_weights.astype(jnp.bfloat16),
        new_values,
        preferred_element_type=jnp.float32,
    )
    attended = (
        (numerator / denominator[..., None])
        .transpose(0, 3, 1, 2, 4)
        .reshape(seq_count * step_count, heads_local * head_dim)
        .astype(jnp.bfloat16)
    )
    projected = of_everyone(jnp.dot(attended, out_weight, preferred_element_type=jnp.float32), "tp")
    after_attention = (residual.astype(jnp.float32) + projected).astype(jnp.bfloat16)
    wide_rows = after_attention.astype(jnp.float32)
    model_width = norm_gain.shape[0] * lax.axis_size("kv")
    squares = of_everyone(jnp.sum(wide_rows * wide_rows, axis=1), "kv")
    inverse = lax.rsqrt(squares / model_width + 1e-05)
    normed = (wide_rows * norm_gain.astype(jnp.float32)[None, :] * inverse[:, None]).astype(
        jnp.bfloat16
    )
    gate_part = jnp.dot(normed, gate_weight, preferred_element_type=jnp.float32)
    up_part = jnp.dot(normed, up_weight, preferred_element_type=jnp.float32)
    gate_share, up_share = side_by_side((gate_part, up_part), "kv", 1, 0)
    hidden = collect((jax.nn.silu(gate_share) * up_share).astype(jnp.bfloat16), "kv", 1)
    rows_own = hidden.shape[0] // lax.axis_size("tp")
    own_sums = summed_on_arrival(
        jnp.dot(hidden, down_weight, preferred_element_type=jnp.float32), "tp", 0
    )
    residual_rows = lax.dynamic_slice_in_dim(
        wide_rows, lax.axis_index("tp") * rows_own, rows_own, 0
    )
    return (after_attention, (residual_rows + own_sums).astype(jnp.bfloat16))


def solution(mesh):
    return jax.shard_map(
        local,
        mesh=mesh,
        in_specs=(
            P(None, None, "tp", None),
            P(None, "kv", "tp", None),
            P(None, "kv", "tp", None),
            P(None, None, "tp", None),
            P(None, None, "tp", None),
            P(),
            P(None, "kv"),
            P("tp", "kv"),
            P("kv"),
            P("kv", "tp"),
            P("kv", "tp"),
            P("tp", "kv"),
        ),
        out_specs=(P(None, "kv"), P("tp", "kv")),
        check_vma=False,
    )
```

profile of v0, /device:TPU:1, one launch (start us, length us, event | category | flops | bytes accessed | tf_op | source)
XLA Modules:
  0.0 220.3 jit_solution(5743829172851007249)
XLA Ops:
  0.7 0.9 broadcast_compare_fusion
  1.6 0.6 copy-done.4
  2.2 2.2 fusion.37
  4.3 0.7 copy.51
  5.1 1.5 all_to_all.35
  6.6 12.2 %all-to-all-start = ((f32[32,1,16]{2,1,0:T(1,128)}), f32[32,1,16]{2,1,0:T(1,128)}, u32[]{:S(2)}, u32[]{:S(2)}) async-start(f32[32,1,16]{2,1,0:T(1,128)} %bitcast.93), calls=%async_computation | async-start | bytes 32768 | tf_op jit(solution)/shard_map/all_to_all | solution.py:107
  18.8 1.9 fusion.13
  20.7 1.5 copy.53
  22.1 1.5 all_to_all.37
  23.7 3.5 %all-to-all-done = f32[32,1,16]{2,1,0:T(1,128)} async-done(((f32[32,1,16]{2,1,0:T(1,128)}), f32[32,1,16]{2,1,0:T(1,128)}, u32[]{:S(2)}, u32[]{:S(2)}) %all-to-all-start) | async-done | bytes 2080 | tf_op jit(solution)/shard_map/all_to_all | solution.py:107
  27.2 5.7 %all-to-all-start.1 = ((f32[32,1,16]{2,1,0:T(1,128)}), f32[32,1,16]{2,1,0:T(1,128)}, u32[]{:S(2)}, u32[]{:S(2)}) async-start(f32[32,1,16]{2,1,0:T(1,128)} %bitcast.92), calls=%async_computation.1 | async-start | bytes 32768 | tf_op jit(solution)/shard_map/all_to_all | solution.py:110
  32.9 1.5 fusion.9
  34.4 0.8 copy.55
  35.2 6.2 %all-to-all-done.1 = f32[32,1,16]{2,1,0:T(1,128)} async-done(((f32[32,1,16]{2,1,0:T(1,128)}), f32[32,1,16]{2,1,0:T(1,128)}, u32[]{:S(2)}, u32[]{:S(2)}) %all-to-all-start.1) | async-done | bytes 2080 | tf_op jit(solution)/shard_map/all_to_all | solution.py:110
  41.5 4.6 %all-to-all-start.2 = ((f32[32,16,128]{2,1,0:T(8,128)}), f32[32,16,128]{2,1,0:T(8,128)}, u32[]{:S(2)}, u32[]{:S(2)}) async-start(f32[32,16,128]{2,1,0:T(8,128)} %bitcast.86), calls=%async_computation.2 | async-start | bytes 524288 | tf_op jit(solution)/shard_map/all_to_all | solution.py:113
  46.1 0.5 copy-done.6
  46.6 1.7 fusion.38
  48.3 0.8 reduce_max.28
  49.2 0.8 multiply_reduce_fusion.2
  50.0 6.6 %all-to-all-done.2 = f32[32,16,128]{2,1,0:T(8,128)} async-done(((f32[32,16,128]{2,1,0:T(8,128)}), f32[32,16,128]{2,1,0:T(8,128)}, u32[]{:S(2)}, u32[]{:S(2)}) %all-to-all-start.2) | async-done | bytes 262176 | tf_op jit(solution)/shard_map/all_to_all | solution.py:113
  56.6 1.1 multiply_reduce_fusion
  57.8 35.3 %all_gather.3 = f32[512,130]{1,0:T(8,128)S(1)} all-gather(f32[16,130]{1,0:T(8,128)S(1)} %pad_maximum_fusion.1), channel_id=1, replica_groups=mesh['kv'=32,'tp'=8] {'kv'}, dimensions={0}, use_global_device_ids=true | all-gather | bytes 274560 | tf_op jit(solution)/shard_map/all_gather | solution.py:11
  93.1 0.3 slice_reduce_fusion
  93.4 0.8 slice.12
  94.7 1.0 fusion.22
  95.7 1.4 fusion.6
  97.1 2.0 fusion.19
  99.2 29.3 %all_to_all.55 = f32[8,32,512]{2,1,0:T(8,128)} all-to-all(f32[8,32,512]{2,1,0:T(8,128)S(1)} %broadcast_in_dim.63), channel_id=1, replica_groups=mesh['kv'=32,'tp'=8] {'tp'}, dimensions={0} | all-to-all | bytes 1048576 | tf_op jit(solution)/shard_map/all_to_all | solution.py:21
  128.5 1.1 reduce_sum.85
  129.6 0.6 fusion.36
  130.3 0.6 broadcast_in_dim.64
  131.0 4.9 %all-to-all-start.4 = ((f32[32,1,32]{2,1,0:T(1,128)}), f32[32,1,32]{2,1,0:T(1,128)S(1)}, u32[]{:S(2)}, u32[]{:S(2)}) async-start(f32[32,1,32]{2,1,0:T(1,128)} %broadcast_in_dim.64), calls=%async_computation.4 | async-start | bytes 32768 | tf_op jit(solution)/shard_map/all_to_all | solution.py:21
  135.9 8.6 %all-to-all-done.4 = f32[32,1,32]{2,1,0:T(1,128)S(1)} async-done(((f32[32,1,32]{2,1,0:T(1,128)}), f32[32,1,32]{2,1,0:T(1,128)S(1)}, u32[]{:S(2)}, u32[]{:S(2)}) %all-to-all-start.4) | async-done | bytes 4128 | tf_op jit(solution)/shard_map/all_to_all | solution.py:21
  144.5 0.7 fusion.30
  145.2 1.2 copy-done.1
  146.4 0.7 fusion.31
  147.2 1.0 pad_maximum_fusion
  148.2 3.4 %reshape.205 = f32[64,32,104]{2,1,0:T(8,128)} reshape(f32[64,3328]{1,0:T(8,128)} %pad_maximum_fusion) | data formatting | bytes 1703936 | tf_op jit(solution)/shard_map/reshape | solution.py:31
  151.6 1.8 copy.78
  153.4 28.8 %all_to_all.56 = f32[32,64,104]{2,1,0:T(8,128)} all-to-all(f32[32,64,104]{2,1,0:T(8,128)S(1)} %bitcast.85), channel_id=1, replica_groups=mesh['kv'=32,'tp'=8] {'kv'}, dimensions={0} | all-to-all | bytes 1703936 | tf_op jit(solution)/shard_map/all_to_all | solution.py:36
  182.2 1.3 reduce_sum.88
  183.6 17.1 %all_to_all.57 = bf16[32,32,104]{2,1,0:T(8,128)(2,1)S(1)} all-to-all(bf16[32,32,104]{2,1,0:T(8,128)(2,1)S(1)} %broadcast_in_dim.65), channel_id=1, replica_groups=mesh['kv'=32,'tp'=8] {'kv'}, dimensions={0} | all-to-all | bytes 425984 | tf_op jit(solution)/shard_map/all_to_all | solution.py:21
  200.7 0.8 copy.64
  201.5 2.1 dot_general.33
  203.6 3.3 %fusion = f32[8,4,512]{2,1,0:T(4,128)} fusion(bf16[8,4,3328]{2,1,0:T(4,128)(2,1)} %dot_general.33, bf16[3328,512]{1,0:T(8,128)(2,1)} %param.23), kind=kOutput, calls=%fused_computation | convolution fusion | flops 109051904 | bytes 3686400 | tf_op jit(solution)/shard_map/dot_general | solution.py:165
  207.0 7.1 %all-to-all-start.7 = ((f32[8,4,512]{2,1,0:T(4,128)}), f32[8,4,512]{2,1,0:T(4,128)S(1)}, u32[]{:S(2)}, u32[]{:S(2)}) async-start(f32[8,4,512]{2,1,0:T(4,128)} %fusion), calls=%async_computation.7 | async-start | bytes 131072 | tf_op jit(solution)/shard_map/all_to_all | solution.py:36
  214.1 4.9 %all-to-all-done.7 = f32[8,4,512]{2,1,0:T(4,128)S(1)} async-done(((f32[8,4,512]{2,1,0:T(4,128)}), f32[8,4,512]{2,1,0:T(4,128)S(1)}, u32[]{:S(2)}, u32[]{:S(2)}) %all-to-all-start.7) | async-done | bytes 65568 | tf_op jit(solution)/shard_map/all_to_all | solution.py:36
  219.0 1.3 add_convert_fusion.1
  (32 shorter events, 1.0 us)
Async XLA Ops:
  0.6 143.9 %copy-start = (bf16[512,3328]{1,0:T(8,128)(2,1)S(1)}, bf16[512,3328]{1,0:T(8,128)(2,1)}, u32[]{:S(2)}) copy-start(bf16[512,3328]{1,0:T(8,128)(2,1)} %param.22) | copy-start | bytes 10223620
  0.6 45.9 %copy-start.3 = (bf16[8,4,16,128]{3,2,1,0:T(8,128)(2,1)S(1)}, bf16[8,4,16,128]{3,2,1,0:T(8,128)(2,1)}, u32[]{:S(2)}) copy-start(bf16[8,4,16,128]{3,2,1,0:T(8,128)(2,1)} %param.12) | copy-start | bytes 393220
  1.6 0.6 copy-start.4
  6.6 20.6 %all-to-all-start = ((f32[32,1,16]{2,1,0:T(1,128)}), f32[32,1,16]{2,1,0:T(1,128)}, u32[]{:S(2)}, u32[]{:S(2)}) async-start(f32[32,1,16]{2,1,0:T(1,128)} %bitcast.93), calls=%async_computation | async-start | bytes 32768 | tf_op jit(solution)/shard_map/all_to_all | solution.py:107
  27.2 14.3 %all-to-all-start.1 = ((f32[32,1,16]{2,1,0:T(1,128)}), f32[32,1,16]{2,1,0:T(1,128)}, u32[]{:S(2)}, u32[]{:S(2)}) async-start(f32[32,1,16]{2,1,0:T(1,128)} %bitcast.92), calls=%async_computation.1 | async-start | bytes 32768 | tf_op jit(solution)/shard_map/all_to_all | solution.py:110
  41.5 15.2 %all-to-all-start.2 = ((f32[32,16,128]{2,1,0:T(8,128)}), f32[32,16,128]{2,1,0:T(8,128)}, u32[]{:S(2)}, u32[]{:S(2)}) async-start(f32[32,16,128]{2,1,0:T(8,128)} %bitcast.86), calls=%async_computation.2 | async-start | bytes 524288 | tf_op jit(solution)/shard_map/all_to_all | solution.py:113
  46.1 0.5 copy-start.6
  94.2 35.3 %copy-start.5 = (bf16[32,512]{1,0:T(8,128)(2,1)S(1)}, bf16[32,512]{1,0:T(8,128)(2,1)}, u32[]{:S(2)}) copy-start(bf16[32,512]{1,0:T(8,128)(2,1)} %param.18) | copy-start | bytes 98308
  94.7 41.1 %copy-start.7 = (bf16[512]{0:T(512)(128)(2,1)S(1)}, bf16[512]{0:T(512)(128)(2,1)}, u32[]{:S(2)}) copy-start(bf16[512]{0:T(512)(128)(2,1)} %param.20) | copy-start | bytes 3076
  130.2 16.9 %copy-start.2 = (bf16[32,512]{1,0:T(8,128)(2,1)}, bf16[32,512]{1,0:T(8,128)(2,1)S(1)}, u32[]{:S(2)}) copy-start(bf16[32,512]{1,0:T(8,128)(2,1)S(1)} %get-tuple-element.5) | copy-start | bytes 98308
  131.0 13.5 %all-to-all-start.4 = ((f32[32,1,32]{2,1,0:T(1,128)}), f32[32,1,32]{2,1,0:T(1,128)S(1)}, u32[]{:S(2)}, u32[]{:S(2)}) async-start(f32[32,1,32]{2,1,0:T(1,128)} %broadcast_in_dim.64), calls=%async_computation.4 | async-start | bytes 32768 | tf_op jit(solution)/shard_map/all_to_all | solution.py:21
  144.5 2.0 copy-start.1
  207.0 12.0 %all-to-all-start.7 = ((f32[8,4,512]{2,1,0:T(4,128)}), f32[8,4,512]{2,1,0:T(4,128)S(1)}, u32[]{:S(2)}, u32[]{:S(2)}) async-start(f32[8,4,512]{2,1,0:T(4,128)} %fusion), calls=%async_computation.7 | async-start | bytes 131072 | tf_op jit(solution)/shard_map/all_to_all | solution.py:36
where the time goes:
time: 222 us; the launch traced here: 220 us
  blocking collectives  110 us (50%)
  starting transfers between devices  34.5 us (16%)
  waiting for transfers between devices  29.8 us (13%)
  local copies, waits for them, and re-layouts  19 us (9%)
  matrix products  13.6 us (6%)
  other arithmetic  12.1 us (5%)
    all_to_all x2, blocking collectives, sent_to_all(): return lax.all_to_all(copies, axis, split_axis=0, concat_axis=0, tiled=True)  46.4 us
    all_gather x1, blocking collectives, turned_gather(): result, at, done = (lax.all_gather(both, axis, axis=0, tiled=True), 0, [])  35.3 us
    all_to_all x1, blocking collectives, summed_on_arrival(): tiles = lax.all_to_all(split_up(array, dim, peers), axis, 0, 0, tiled=True)  28.8 us
    all_to_all x1, starting transfers between devices, local(): lax.all_to_all(local_max.reshape(pieces, -1), 'kv', split_axis=0, concat_...  12.2 us
    all_to_all x1, waiting for transfers between devices, sent_to_all(): return lax.all_to_all(copies, axis, split_axis=0, concat_axis=0, tiled=True)  8.6 us
    all_to_all x1, starting transfers between devices, summed_on_arrival(): tiles = lax.all_to_all(split_up(array, dim, peers), axis, 0, 0, tiled=True)  7.12 us
    all_to_all x1, waiting for transfers between devices, local(): lax.all_to_all(local_sum.reshape(pieces, -1, head_dim), 'kv', split_axis=...  6.58 us
    all_to_all x1, waiting for transfers between devices, local(): lax.all_to_all(local_total.reshape(pieces, -1), 'kv', split_axis=0, conca...  6.2 us
  transfers between devices with their start and end apart: 5, of which 5 were waited for; matrix products, arithmetic and copies ran while one was open for 4% of the time, Pallas kernels for 0%

commit v1 on v0

--- a/solution.py
+++ b/solution.py
@@ -5,10 +5,15 @@
 from jax.sharding import PartitionSpec as P
 
 
+def gather_over(array, axis, along):
+    stack = jnp.stack([array] * lax.axis_size(axis))
+    return jnp.concatenate(lax.all_to_all(stack, axis, 0, 0), axis=along)
+
+
 def turned_gather(arrays, axis, dims):
     turned = [jnp.moveaxis(a, dim, 0) for a, dim in zip(arrays, dims)]
     both = jnp.concatenate([t.reshape(len(t), -1) for t in turned], axis=1)
-    result, at, done = (lax.all_gather(both, axis, axis=0, tiled=True), 0, [])
+    result, at, done = (gather_over(both, axis, 0), 0, [])
     for t, dim in zip(turned, dims):
         piece = result[:, at : at + t[0].size].reshape(-1, *t.shape[1:])
         done.append(jnp.moveaxis(piece, 0, dim))

time: 222 us -> 197 us (0.89)
  blocking collectives: 110 us -> 65.2 us
  waiting for transfers between devices: 29.8 us -> 40.5 us
  local copies, waits for them, and re-layouts: 19 us -> 23.8 us
  starting transfers between devices: 34.5 us -> 38.3 us
    all_gather x1 -> x0, blocking collectives: 35.3 us -> none  [turned_gather(): result, at, done = (lax.all_gather(both, axis, axis=0, tiled=True), 0, [])]
    all_to_all x0 -> x1, waiting for transfers between devices: none -> 10.8 us  [gather_over(): return jnp.concatenate(lax.all_to_all(stack, axis, 0, 0), axis=along)]
    all_to_all x2, blocking collectives: 46.4 us -> 36.4 us  [sent_to_all(): return lax.all_to_all(copies, axis, split_axis=0, concat_axis=0, tiled=True)]
    all_to_all x0 -> x1, starting transfers between devices: none -> 4.61 us  [gather_over(): return jnp.concatenate(lax.all_to_all(stack, axis, 0, 0), axis=along)]
  transfers between devices with their start and end apart: 5 -> 6, of which waited for: 5 -> 6; matrix products, arithmetic and copies ran while one was open for 4% -> 6% of each run, Pallas kernels for 0% -> 0%
where the time goes in v1:
time: 197 us; the launch traced here: 196 us
  blocking collectives  65.2 us (33%)
  waiting for transfers between devices  40.5 us (21%)
  starting transfers between devices  38.3 us (19%)
  local copies, waits for them, and re-layouts  23.8 us (12%)
  matrix products  13.6 us (7%)
  other arithmetic  13.4 us (7%)
    all_to_all x2, blocking collectives, sent_to_all(): return lax.all_to_all(copies, axis, split_axis=0, concat_axis=0, tiled=True)  36.4 us
    all_to_all x1, blocking collectives, summed_on_arrival(): tiles = lax.all_to_all(split_up(array, dim, peers), axis, 0, 0, tiled=True)  28.8 us
    all_to_all x1, starting transfers between devices, local(): lax.all_to_all(local_max.reshape(pieces, -1), 'kv', split_axis=0, concat_...  12.2 us
    all_to_all x1, waiting for transfers between devices, gather_over(): return jnp.concatenate(lax.all_to_all(stack, axis, 0, 0), axis=along)  10.8 us
    all_to_all x1, waiting for transfers between devices, sent_to_all(): return lax.all_to_all(copies, axis, split_axis=0, concat_axis=0, tiled=True)  8.6 us
    all_to_all x1, starting transfers between devices, summed_on_arrival(): tiles = lax.all_to_all(split_up(array, dim, peers), axis, 0, 0, tiled=True)  7.11 us
    all_to_all x1, waiting for transfers between devices, local(): lax.all_to_all(local_sum.reshape(pieces, -1, head_dim), 'kv', split_axis=...  6.42 us
    all_to_all x1, waiting for transfers between devices, local(): lax.all_to_all(local_total.reshape(pieces, -1), 'kv', split_axis=0, conca...  6.2 us
  transfers between devices with their start and end apart: 6, of which 6 were waited for; matrix products, arithmetic and copies ran while one was open for 6% of the time, Pallas kernels for 0%

profile of v1, /device:TPU:1, one launch (start us, length us, event | category | flops | bytes accessed | tf_op | source)
XLA Modules:
  0.0 195.6 jit_solution(7530040644546533926)
XLA Ops:
  0.7 0.9 broadcast_compare_fusion
  2.2 2.2 %fusion.37 = (f32[8,16,4]{1,2,0:T(4,128)S(1)}, f32[8,1,16,4,256]{4,2,3,0,1:T(8,128)}) fusion(bf16[8,4,16,128]{3,2,1,0:T(8,128)(2,1)} %param.12, bf16[8,256,1,128]{3,1,2,0:T(8,128)(2,1)} %param.13, pred[8,256]{1,0:T(8,128)(4,1)S(1)} %broadcast_compare_fusion), kind=kOutput, calls=%fused_computation.60 | convolution fusion | flops 33947136 | bytes 1183744 | tf_op jit(solution)/shard_map/stgjd,scgd->sgjtc/dot_general | solution.py:94
  4.3 0.7 copy.51
  5.1 1.5 all_to_all.38
  6.6 12.2 %all-to-all-start = ((f32[32,1,16]{2,1,0:T(1,128)}), f32[32,1,16]{2,1,0:T(1,128)}, u32[]{:S(2)}, u32[]{:S(2)}) async-start(f32[32,1,16]{2,1,0:T(1,128)} %bitcast.94), calls=%async_computation | async-start | bytes 32768 | tf_op jit(solution)/shard_map/all_to_all | solution.py:112
  18.8 1.9 fusion.13
  20.7 1.5 copy.53
  22.1 1.5 all_to_all.40
  23.7 3.5 %all-to-all-done = f32[32,1,16]{2,1,0:T(1,128)} async-done(((f32[32,1,16]{2,1,0:T(1,128)}), f32[32,1,16]{2,1,0:T(1,128)}, u32[]{:S(2)}, u32[]{:S(2)}) %all-to-all-start) | async-done | bytes 2080 | tf_op jit(solution)/shard_map/all_to_all | solution.py:112
  27.2 5.7 %all-to-all-start.1 = ((f32[32,1,16]{2,1,0:T(1,128)}), f32[32,1,16]{2,1,0:T(1,128)}, u32[]{:S(2)}, u32[]{:S(2)}) async-start(f32[32,1,16]{2,1,0:T(1,128)} %bitcast.93), calls=%async_computation.1 | async-start | bytes 32768 | tf_op jit(solution)/shard_map/all_to_all | solution.py:115
  32.9 1.5 fusion.9
  34.4 0.8 copy.55
  35.2 6.2 %all-to-all-done.1 = f32[32,1,16]{2,1,0:T(1,128)} async-done(((f32[32,1,16]{2,1,0:T(1,128)}), f32[32,1,16]{2,1,0:T(1,128)}, u32[]{:S(2)}, u32[]{:S(2)}) %all-to-all-start.1) | async-done | bytes 2080 | tf_op jit(solution)/shard_map/all_to_all | solution.py:115
  41.5 4.6 %all-to-all-start.2 = ((f32[32,16,128]{2,1,0:T(8,128)}), f32[32,16,128]{2,1,0:T(8,128)}, u32[]{:S(2)}, u32[]{:S(2)}) async-start(f32[32,16,128]{2,1,0:T(8,128)} %bitcast.87), calls=%async_computation.2 | async-start | bytes 524288 | tf_op jit(solution)/shard_map/all_to_all | solution.py:118
  46.1 0.8 reduce_max.28
  47.5 1.3 multiply_reduce_fusion.2
  48.8 1.3 copy.57
  50.2 6.4 %all-to-all-done.2 = f32[32,16,128]{2,1,0:T(8,128)} async-done(((f32[32,16,128]{2,1,0:T(8,128)}), f32[32,16,128]{2,1,0:T(8,128)}, u32[]{:S(2)}, u32[]{:S(2)}) %all-to-all-start.2) | async-done | bytes 262176 | tf_op jit(solution)/shard_map/all_to_all | solution.py:118
  56.6 1.1 multiply_reduce_fusion
  57.7 0.8 pad_maximum_fusion.1
  58.5 0.9 stack.2
  59.4 4.6 %all-to-all-start.3 = ((f32[32,16,130]{2,1,0:T(8,128)}), f32[32,16,130]{2,1,0:T(8,128)}, u32[]{:S(2)}, u32[]{:S(2)}) async-start(f32[32,16,130]{2,1,0:T(8,128)} %stack.2), calls=%async_computation.3 | async-start | bytes 1048576 | tf_op jit(solution)/shard_map/all_to_all | solution.py:10
  64.5 1.7 fusion.38
  66.3 10.8 %all-to-all-done.3 = f32[32,16,130]{2,1,0:T(8,128)} async-done(((f32[32,16,130]{2,1,0:T(8,128)}), f32[32,16,130]{2,1,0:T(8,128)}, u32[]{:S(2)}, u32[]{:S(2)}) %all-to-all-start.3) | async-done | bytes 266272 | tf_op jit(solution)/shard_map/all_to_all | solution.py:10
  77.1 1.3 slice_reduce_fusion
  78.4 1.9 slice.12
  80.8 1.0 fusion.22
  81.8 1.4 fusion.6
  83.2 2.0 %fusion.19 = f32[32,512]{1,0:T(8,128)S(1)} fusion(bf16[2048,512]{1,0:T(8,128)(2,1)} %param.19, bf16[4,8,16,128]{3,2,1,0:T(8,128)(2,1)S(1)} %bitcast.92), kind=kOutput, calls=%fused_computation.28 | convolution fusion | flops 67108864 | bytes 2293760 | tf_op jit(solution)/shard_map/dot_general | solution.py:155
  85.3 19.3 %all_to_all.60 = f32[8,32,512]{2,1,0:T(8,128)} all-to-all(f32[8,32,512]{2,1,0:T(8,128)S(1)} %broadcast_in_dim.63), channel_id=1, replica_groups=mesh['kv'=32,'tp'=8] {'tp'}, dimensions={0} | all-to-all | bytes 1048576 | tf_op jit(solution)/shard_map/all_to_all | solution.py:26
  104.6 1.1 reduce_sum.85
  107.1 4.1 %all-to-all-start.5 = ((f32[32,1,32]{2,1,0:T(1,128)}), f32[32,1,32]{2,1,0:T(1,128)S(1)}, u32[]{:S(2)}, u32[]{:S(2)}) async-start(f32[32,1,32]{2,1,0:T(1,128)} %broadcast_in_dim.64), calls=%async_computation.5 | async-start | bytes 32768 | tf_op jit(solution)/shard_map/all_to_all | solution.py:26
  111.2 8.6 %all-to-all-done.5 = f32[32,1,32]{2,1,0:T(1,128)S(1)} async-done(((f32[32,1,32]{2,1,0:T(1,128)}), f32[32,1,32]{2,1,0:T(1,128)S(1)}, u32[]{:S(2)}, u32[]{:S(2)}) %all-to-all-start.5) | async-done | bytes 4128 | tf_op jit(solution)/shard_map/all_to_all | solution.py:26
  119.9 0.7 fusion.30
  120.6 1.2 copy-done.1
  121.8 0.7 fusion.31
  122.5 1.0 pad_maximum_fusion
  123.5 3.4 %reshape.211 = f32[64,32,104]{2,1,0:T(8,128)} reshape(f32[64,3328]{1,0:T(8,128)} %pad_maximum_fusion) | data formatting | bytes 1703936 | tf_op jit(solution)/shard_map/reshape | solution.py:36
  126.9 1.8 copy.78
  128.8 28.8 %all_to_all.61 = f32[32,64,104]{2,1,0:T(8,128)} all-to-all(f32[32,64,104]{2,1,0:T(8,128)S(1)} %bitcast.86), channel_id=1, replica_groups=mesh['kv'=32,'tp'=8] {'kv'}, dimensions={0} | all-to-all | bytes 1703936 | tf_op jit(solution)/shard_map/all_to_all | solution.py:41
  157.5 1.3 reduce_sum.88
  158.9 17.1 %all_to_all.62 = bf16[32,32,104]{2,1,0:T(8,128)(2,1)S(1)} all-to-all(bf16[32,32,104]{2,1,0:T(8,128)(2,1)S(1)} %broadcast_in_dim.65), channel_id=1, replica_groups=mesh['kv'=32,'tp'=8] {'kv'}, dimensions={0} | all-to-all | bytes 425984 | tf_op jit(solution)/shard_map/all_to_all | solution.py:26
  176.0 0.8 copy.64
  176.8 2.1 %dot_general.33 = bf16[8,4,3328]{2,1,0:T(4,128)(2,1)} reshape(bf16[32,32,104]{2,1,0:T(8,128)(2,1)} %copy.64) | data formatting | bytes 425984 | tf_op jit(solution)/shard_map/dot_general | solution.py:170
  179.0 3.4 %fusion = f32[8,4,512]{2,1,0:T(4,128)} fusion(bf16[8,4,3328]{2,1,0:T(4,128)(2,1)} %dot_general.33, bf16[3328,512]{1,0:T(8,128)(2,1)} %param.23), kind=kOutput, calls=%fused_computation | convolution fusion | flops 109051904 | bytes 3686400 | tf_op jit(solution)/shard_map/dot_general | solution.py:170
  182.3 7.1 %all-to-all-start.8 = ((f32[8,4,512]{2,1,0:T(4,128)}), f32[8,4,512]{2,1,0:T(4,128)S(1)}, u32[]{:S(2)}, u32[]{:S(2)}) async-start(f32[8,4,512]{2,1,0:T(4,128)} %fusion), calls=%async_computation.8 | async-start | bytes 131072 | tf_op jit(solution)/shard_map/all_to_all | solution.py:41
  189.4 4.9 %all-to-all-done.8 = f32[8,4,512]{2,1,0:T(4,128)S(1)} async-done(((f32[8,4,512]{2,1,0:T(4,128)}), f32[8,4,512]{2,1,0:T(4,128)S(1)}, u32[]{:S(2)}, u32[]{:S(2)}) %all-to-all-start.8) | async-done | bytes 65568 | tf_op jit(solution)/shard_map/all_to_all | solution.py:41
  194.3 1.3 add_convert_fusion.1
  (36 shorter events, 3.8 us)
Async XLA Ops:
  0.6 119.2 %copy-start = (bf16[512,3328]{1,0:T(8,128)(2,1)S(1)}, bf16[512,3328]{1,0:T(8,128)(2,1)}, u32[]{:S(2)}) copy-start(bf16[512,3328]{1,0:T(8,128)(2,1)} %param.22) | copy-start | bytes 10223620
  0.6 63.9 %copy-start.3 = (bf16[8,4,16,128]{3,2,1,0:T(8,128)(2,1)S(1)}, bf16[8,4,16,128]{3,2,1,0:T(8,128)(2,1)}, u32[]{:S(2)}) copy-start(bf16[8,4,16,128]{3,2,1,0:T(8,128)(2,1)} %param.12) | copy-start | bytes 393220
  1.6 0.6 copy-start.4
  6.6 20.6 %all-to-all-start = ((f32[32,1,16]{2,1,0:T(1,128)}), f32[32,1,16]{2,1,0:T(1,128)}, u32[]{:S(2)}, u32[]{:S(2)}) async-start(f32[32,1,16]{2,1,0:T(1,128)} %bitcast.94), calls=%async_computation | async-start | bytes 32768 | tf_op jit(solution)/shard_map/all_to_all | solution.py:112
  27.2 14.3 %all-to-all-start.1 = ((f32[32,1,16]{2,1,0:T(1,128)}), f32[32,1,16]{2,1,0:T(1,128)}, u32[]{:S(2)}, u32[]{:S(2)}) async-start(f32[32,1,16]{2,1,0:T(1,128)} %bitcast.93), calls=%async_computation.1 | async-start | bytes 32768 | tf_op jit(solution)/shard_map/all_to_all | solution.py:115
  41.5 15.2 %all-to-all-start.2 = ((f32[32,16,128]{2,1,0:T(8,128)}), f32[32,16,128]{2,1,0:T(8,128)}, u32[]{:S(2)}, u32[]{:S(2)}) async-start(f32[32,16,128]{2,1,0:T(8,128)} %bitcast.87), calls=%async_computation.2 | async-start | bytes 524288 | tf_op jit(solution)/shard_map/all_to_all | solution.py:118
  46.8 0.7 copy-start.6
  59.4 17.7 %all-to-all-start.3 = ((f32[32,16,130]{2,1,0:T(8,128)}), f32[32,16,130]{2,1,0:T(8,128)}, u32[]{:S(2)}, u32[]{:S(2)}) async-start(f32[32,16,130]{2,1,0:T(8,128)} %stack.2), calls=%async_computation.3 | async-start | bytes 1048576 | tf_op jit(solution)/shard_map/all_to_all | solution.py:10
  64.0 0.5 copy-start.7
  80.3 25.4 %copy-start.5 = (bf16[32,512]{1,0:T(8,128)(2,1)S(1)}, bf16[32,512]{1,0:T(8,128)(2,1)}, u32[]{:S(2)}) copy-start(bf16[32,512]{1,0:T(8,128)(2,1)} %param.18) | copy-start | bytes 98308
  80.8 30.4 %copy-start.8 = (bf16[512]{0:T(512)(128)(2,1)S(1)}, bf16[512]{0:T(512)(128)(2,1)}, u32[]{:S(2)}) copy-start(bf16[512]{0:T(512)(128)(2,1)} %param.20) | copy-start | bytes 3076
  106.3 16.2 %copy-start.2 = (bf16[32,512]{1,0:T(8,128)(2,1)}, bf16[32,512]{1,0:T(8,128)(2,1)S(1)}, u32[]{:S(2)}) copy-start(bf16[32,512]{1,0:T(8,128)(2,1)S(1)} %get-tuple-element.5) | copy-start | bytes 98308
  107.1 12.8 %all-to-all-start.5 = ((f32[32,1,32]{2,1,0:T(1,128)}), f32[32,1,32]{2,1,0:T(1,128)S(1)}, u32[]{:S(2)}, u32[]{:S(2)}) async-start(f32[32,1,32]{2,1,0:T(1,128)} %broadcast_in_dim.64), calls=%async_computation.5 | async-start | bytes 32768 | tf_op jit(solution)/shard_map/all_to_all | solution.py:26
  119.8 2.0 %copy-start.1 = (bf16[512,3328]{1,0:T(8,128)(2,1)S(1)}, bf16[512,3328]{1,0:T(8,128)(2,1)}, u32[]{:S(2)}) copy-start(bf16[512,3328]{1,0:T(8,128)(2,1)} %param.21) | copy-start | bytes 10223620
  182.3 12.0 %all-to-all-start.8 = ((f32[8,4,512]{2,1,0:T(4,128)}), f32[8,4,512]{2,1,0:T(4,128)S(1)}, u32[]{:S(2)}, u32[]{:S(2)}) async-start(f32[8,4,512]{2,1,0:T(4,128)} %fusion), calls=%async_computation.8 | async-start | bytes 131072 | tf_op jit(solution)/shard_map/all_to_all | solution.py:41
